TPU v7x, 32 devices: a whole 2x2x4 slice. The times are simulated.
32 devices in a mesh: dp: 8 (over z, x), tp: 4 (over y, core).
Axes of the slice: x: 2, y: 2, z: 4, core: 2. Of those that a mesh axis runs over, the one named last changes fastest.
Arguments:
- inputs: bfloat16 [2, 4096, 768], P(None, 'dp'), may hold values from -6 to 6
- cotangent: bfloat16 [2, 4096, 768], P(None, 'dp'), may hold values from -6 to 6
- item_ids: int32 [2, 4096], P(None, 'dp'), may hold values from 0 to 3584, as said below
- timestep: int32 [2, 8], P(None, 'dp'), may hold values from 0 to 999
- qkv_weight: float32 [768, 3, 768], P('dp', None, 'tp'), may hold values from -0.21875 to 0.21875
- out_weight: float32 [768, 768], P('tp', 'dp'), may hold values from -0.625 to 0.625
- up_weight: float32 [768, 3072], P('dp', 'tp'), may hold values from -0.21875 to 0.21875
- down_weight: float32 [3072, 768], P('tp', 'dp'), may hold values from -0.109375 to 0.109375
- norm_params: float32 [4, 768], P(None, 'dp')
- qkv_first: float32 [768, 3, 768], P('dp', None, 'tp'), may hold values from -0.00061035156 to 0.00061035156
- out_first: float32 [768, 768], P('tp', 'dp'), may hold values from -0.00061035156 to 0.00061035156
- up_first: float32 [768, 3072], P('dp', 'tp'), may hold values from -0.00061035156 to 0.00061035156
- down_first: float32 [3072, 768], P('tp', 'dp'), may hold values from -0.00061035156 to 0.00061035156
- norm_first: float32 [4, 768], P(None, 'dp'), may hold values from -0.001953125 to 0.001953125
- qkv_second: float32 [768, 3, 768], P('dp', None, 'tp'), may hold values from 1.4122378e-10 to 5.6489513e-10
- out_second: float32 [768, 768], P('tp', 'dp'), may hold values from 1.4122378e-10 to 5.6489513e-10
- up_second: float32 [768, 3072], P('dp', 'tp'), may hold values from 1.4122378e-10 to 5.6489513e-10
- down_second: float32 [3072, 768], P('tp', 'dp'), may hold values from 1.4122378e-10 to 5.6489513e-10
- norm_second: float32 [4, 768], P(None, 'dp'), may hold values from 1.4122379e-09 to 5.6489515e-09
Outputs:
- block_out: bfloat16 [2, 4096, 768], P(None, 'dp')
- input_grad: float32 [2, 4096, 768], P(None, 'dp')
- grad_norm: float32 [], replicated
- qkv_new: float32 [768, 3, 768], P('dp', None, 'tp')
- qkv_first_new: float32 [768, 3, 768], P('dp', None, 'tp')
- qkv_second_new: float32 [768, 3, 768], P('dp', None, 'tp')
- out_new: float32 [768, 768], P('tp', 'dp')
- out_first_new: float32 [768, 768], P('tp', 'dp')
- out_second_new: float32 [768, 768], P('tp', 'dp')
- up_new: float32 [768, 3072], P('dp', 'tp')
- up_first_new: float32 [768, 3072], P('dp', 'tp')
- up_second_new: float32 [768, 3072], P('dp', 'tp')
- down_new: float32 [3072, 768], P('tp', 'dp')
- down_first_new: float32 [3072, 768], P('tp', 'dp')
- down_second_new: float32 [3072, 768], P('tp', 'dp')
- norm_new: float32 [4, 768], P(None, 'dp')
- norm_first_new: float32 [4, 768], P(None, 'dp')
- norm_second_new: float32 [4, 768], P(None, 'dp')
Inputs may be any that keep to these rules, and one draw needn't show every extreme that they name: `item_ids`: A token's id is the index, within its micro-batch, of its item's first token, so ids never decrease along a micro-batch; every block of 512 tokens of one index of dp starts a new item, so no item spans two blocks; an item has 1 to 512 tokens and in every draw some item has exactly 512.
All inputs are finite; a program needn't handle non-finite values.
Results may differ from a plain program's by a relative error of at most 0.009.
Values may be sent and summed in bfloat16 or wider, within the bound.
A program may use at most 128 MiB of HBM per device.

v0:
```python
from functools import partial
import math
import jax
import jax.numpy as jnp
from jax import lax
from jax.sharding import PartitionSpec as P

HEAD_DIM = 64
STEP = 10
norm_eps = 1e-05
clip_limit = 1.0
learn_rate = 0.02
beta_one = 0.9
beta_two = 0.999
adam_eps = 1e-08
weight_decay = 0.01


def time_embed(step_values, model_width):
    half_width = model_width // 2
    frequency = jnp.exp(
        jnp.arange(half_width, dtype=jnp.float32) * (-math.log(10000.0) / half_width)
    )
    angles = step_values.astype(jnp.float32)[..., None] * frequency
    return jnp.concatenate([jnp.sin(angles), jnp.cos(angles)], axis=-1)


def layer_norm(values, gain_row, bias_row):
    centre = values - jnp.mean(values, axis=-1, keepdims=True)
    spread = jnp.mean(centre * centre, axis=-1, keepdims=True)
    return centre * lax.rsqrt(spread + norm_eps) * gain_row + bias_row


def masked_scores(query_rows, key_rows, same_item, score_scale):
    scores = (
        jnp.einsum("thd,shd->hts", query_rows, key_rows, preferred_element_type=jnp.float32)
        * score_scale
    )
    return jnp.where(same_item, scores, -1e30)


def one_micro(gathered, stream_in, upstream, labels, embed_row):
    qkv_mat, out_mat, up_mat, down_mat, norm_rows = gathered
    tokens_here = stream_in.shape[0]
    local_width = out_mat.shape[0]
    heads_here = local_width // HEAD_DIM
    score_scale = 1.0 / math.sqrt(HEAD_DIM)
    split_shape = (tokens_here, heads_here, HEAD_DIM)
    norm_gains = norm_rows.astype(jnp.float32)
    gain_one = 1.0 + norm_gains[0]
    gain_two = 1.0 + norm_gains[2]
    stream = stream_in.astype(jnp.float32) + embed_row[None, :]
    normed_f, norm_one_back = jax.vjp(layer_norm, stream, gain_one, norm_gains[1])
    normed = normed_f.astype(jnp.bfloat16)
    triple = jnp.einsum("td,dje->jte", normed, qkv_mat, preferred_element_type=jnp.float32).astype(
        jnp.bfloat16
    )
    query_rows = triple[0].reshape(split_shape)
    key_rows = triple[1].reshape(split_shape)
    value_rows = triple[2].reshape(split_shape)
    same_item = (labels[:, None] == labels[None, :])[None]
    scores = masked_scores(query_rows, key_rows, same_item, score_scale)
    row_top = jnp.max(scores, axis=-1, keepdims=True)
    exp_scores = jnp.exp(scores - row_top)
    row_total = jnp.sum(exp_scores, axis=-1, keepdims=True)
    probs_soft = exp_scores / row_total
    log_total = row_top + jnp.log(row_total)
    context = (
        jnp.einsum(
            "hts,shd->thd",
            probs_soft.astype(jnp.bfloat16),
            value_rows,
            preferred_element_type=jnp.float32,
        )
        .reshape(tokens_here, local_width)
        .astype(jnp.bfloat16)
    )
    attn_out = lax.psum(jnp.dot(context, out_mat, preferred_element_type=jnp.float32), "tp")
    middle = stream + attn_out
    normed_two_f, norm_two_back = jax.vjp(layer_norm, middle, gain_two, norm_gains[3])
    normed_two = normed_two_f.astype(jnp.bfloat16)
    hidden_pre = jnp.dot(normed_two, up_mat, preferred_element_type=jnp.float32)
    hidden_f, gelu_back = jax.vjp(partial(jax.nn.gelu, approximate=False), hidden_pre)
    hidden = hidden_f.astype(jnp.bfloat16)
    branch = lax.psum(
        jnp.dot(hidden, down_mat, preferred_element_type=jnp.float32).astype(jnp.bfloat16), "tp"
    ).astype(jnp.float32)
    block_out = (middle + branch).astype(jnp.bfloat16)
    grad_down = jnp.einsum("tf,td->fd", hidden, upstream, preferred_element_type=jnp.float32)
    grad_hidden = jnp.einsum("td,fd->tf", upstream, down_mat, preferred_element_type=jnp.float32)
    grad_pre = gelu_back(grad_hidden)[0].astype(jnp.bfloat16)
    grad_up = jnp.einsum("td,tf->df", normed_two, grad_pre, preferred_element_type=jnp.float32)
    grad_normed_two = lax.psum(
        jnp.einsum("tf,df->td", grad_pre, up_mat, preferred_element_type=jnp.float32), "tp"
    )
    grad_middle_norm, grad_gain_two, grad_bias_two = norm_two_back(grad_normed_two)
    grad_middle = upstream.astype(jnp.float32) + grad_middle_norm
    grad_attn = grad_middle.astype(jnp.bfloat16)
    grad_outmat = jnp.einsum("tc,td->cd", context, grad_attn, preferred_element_type=jnp.float32)
    grad_context = (
        jnp.einsum("td,cd->tc", grad_attn, out_mat, preferred_element_type=jnp.float32)
        .astype(jnp.bfloat16)
        .reshape(split_shape)
    )
    probs_again = jnp.exp(masked_scores(query_rows, key_rows, same_item, score_scale) - log_total)
    grad_values = jnp.einsum(
        "hts,thd->shd",
        probs_again.astype(jnp.bfloat16),
        grad_context,
        preferred_element_type=jnp.float32,
    )
    grad_probs = jnp.einsum(
        "thd,shd->hts", grad_context, value_rows, preferred_element_type=jnp.float32
    )
    inner_sum = jnp.sum(grad_probs * probs_again, axis=-1, keepdims=True)
    grad_scores = (probs_again * (grad_probs - inner_sum)).astype(jnp.bfloat16)
    grad_query = (
        jnp.einsum("hts,shd->thd", grad_scores, key_rows, preferred_element_type=jnp.float32)
        * score_scale
    )
    grad_key = (
        jnp.einsum("hts,thd->shd", grad_scores, query_rows, preferred_element_type=jnp.float32)
        * score_scale
    )
    grad_triple = (
        jnp.stack([grad_query, grad_key, grad_values])
        .reshape(3, tokens_here, local_width)
        .astype(jnp.bfloat16)
    )
    grad_qkv = jnp.einsum("td,jte->dje", normed, grad_triple, preferred_element_type=jnp.float32)
    grad_normed = lax.psum(
        jnp.einsum("jte,dje->td", grad_triple, qkv_mat, preferred_element_type=jnp.float32).astype(
            jnp.bfloat16
        ),
        "tp",
    ).astype(jnp.float32)
    grad_stream_norm, grad_gain_one, grad_bias_one = norm_one_back(grad_normed)
    grad_input = grad_middle + grad_stream_norm
    grad_norms = jnp.stack([grad_gain_one, grad_bias_one, grad_gain_two, grad_bias_two])
    return (block_out, grad_input, (grad_qkv, grad_outmat, grad_up, grad_down, grad_norms))


def adam_step(weight, gradient, first_old, second_old):
    first_new = beta_one * first_old + (1.0 - beta_one) * gradient
    second_new = beta_two * second_old + (1.0 - beta_two) * gradient * gradient
    moment_one = first_new / (1.0 - beta_one**STEP)
    moment_two = second_new / (1.0 - beta_two**STEP)
    weight_new = weight - learn_rate * (
        moment_one / (jnp.sqrt(moment_two) + adam_eps) + weight_decay * weight
    )
    return (weight_new, first_new, second_new)


def local(
    inputs,
    cotangent,
    item_ids,
    timestep,
    qkv_weight,
    out_weight,
    up_weight,
    down_weight,
    norm_params,
    qkv_first,
    out_first,
    up_first,
    down_first,
    norm_first,
    qkv_second,
    out_second,
    up_second,
    down_second,
    norm_second,
):
    micro_count = inputs.shape[0]
    embeds = time_embed(timestep[:, 0], inputs.shape[2])
    qkv_low = qkv_weight.astype(jnp.bfloat16)
    out_low = out_weight.astype(jnp.bfloat16)
    up_low = up_weight.astype(jnp.bfloat16)
    down_low = down_weight.astype(jnp.bfloat16)
    norm_low = norm_params.astype(jnp.bfloat16)
    block_list = []
    input_list = []
    for number in range(micro_count):
        gathered = (
            lax.all_gather(qkv_low, "dp", axis=0, tiled=True),
            lax.all_gather(out_low, "dp", axis=1, tiled=True),
            lax.all_gather(up_low, "dp", axis=0, tiled=True),
            lax.all_gather(down_low, "dp", axis=1, tiled=True),
            lax.all_gather(norm_low, "dp", axis=1, tiled=True),
        )
        block_out, grad_input, grad_list = one_micro(
            gathered, inputs[number], cotangent[number], item_ids[number], embeds[number]
        )
        owned_grads = (
            lax.psum_scatter(grad_list[0], "dp", scatter_dimension=0, tiled=True),
            lax.psum_scatter(grad_list[1], "dp", scatter_dimension=1, tiled=True),
            lax.psum_scatter(grad_list[2], "dp", scatter_dimension=0, tiled=True),
            lax.psum_scatter(grad_list[3], "dp", scatter_dimension=1, tiled=True),
            lax.psum_scatter(grad_list[4], "dp", scatter_dimension=1, tiled=True),
        )
        if number == 0:
            totals = tuple(owned_grads)
        else:
            totals = tuple((left + right for left, right in zip(totals, owned_grads)))
        block_list.append(block_out)
        input_list.append(grad_input)
    own_squares = jnp.sum(totals[0] * totals[0]) + jnp.sum(totals[1] * totals[1])
    own_squares = own_squares + jnp.sum(totals[2] * totals[2]) + jnp.sum(totals[3] * totals[3])
    norm_squares = jnp.sum(totals[4] * totals[4])
    own_squares = own_squares + jnp.where(
        lax.axis_index("tp") == 0, norm_squares, jnp.zeros_like(norm_squares)
    )
    grad_norm = jnp.sqrt(lax.psum(own_squares, ("dp", "tp")))
    factor = jnp.minimum(1.0, clip_limit / (grad_norm + 1e-06))
    weights = (qkv_weight, out_weight, up_weight, down_weight, norm_params)
    firsts = (qkv_first, out_first, up_first, down_first, norm_first)
    seconds = (qkv_second, out_second, up_second, down_second, norm_second)
    result = [
        adam_step(weights[index], totals[index] * factor, firsts[index], seconds[index])
        for index in range(5)
    ]
    return (
        jnp.stack(block_list),
        jnp.stack(input_list),
        grad_norm,
        result[0][0],
        result[0][1],
        result[0][2],
        result[1][0],
        result[1][1],
        result[1][2],
        result[2][0],
        result[2][1],
        result[2][2],
        result[3][0],
        result[3][1],
        result[3][2],
        result[4][0],
        result[4][1],
        result[4][2],
    )


def solution(mesh):
    return jax.shard_map(
        local,
        mesh=mesh,
        in_specs=(
            P(None, "dp", None),
            P(None, "dp", None),
            P(None, "dp"),
            P(None, "dp"),
            P("dp", None, "tp"),
            P("tp", "dp"),
            P("dp", "tp"),
            P("tp", "dp"),
            P(None, "dp"),
            P("dp", None, "tp"),
            P("tp", "dp"),
            P("dp", "tp"),
            P("tp", "dp"),
            P(None, "dp"),
            P("dp", None, "tp"),
            P("tp", "dp"),
            P("dp", "tp"),
            P("tp", "dp"),
            P(None, "dp"),
        ),
        out_specs=(
            P(None, "dp", None),
            P(None, "dp", None),
            P(),
            P("dp", None, "tp"),
            P("dp", None, "tp"),
            P("dp", None, "tp"),
            P("tp", "dp"),
            P("tp", "dp"),
            P("tp", "dp"),
            P("dp", "tp"),
            P("dp", "tp"),
            P("dp", "tp"),
            P("tp", "dp"),
            P("tp", "dp"),
            P("tp", "dp"),
            P(None, "dp"),
            P(None, "dp"),
            P(None, "dp"),
        ),
        check_vma=False,
    )
```

profile of v0, /device:TPU:0, one launch (start us, length us, event | category | flops | bytes accessed | tf_op | source)
XLA Modules:
  0.0 723.9 jit_solution(8021237277195858394)
XLA Ops:
  9.0 1.8 fusion.30
  10.9 1.2 fusion.37
  12.2 22.2 %all-gather = bf16[8,96,4]{1,2,0:T(4,128)(2,1)S(1)} all-gather(bf16[1,96,4]{1,2,0:T(4,128)(2,1)S(1)} %convert_bitcast_fusion.2), channel_id=1, replica_groups=mesh['dp'=8,'tp'=4] {'dp'}, dimensions={0}, use_global_device_ids=true | all-gather | bytes 6912 | tf_op jit(solution)/shard_map/all_gather | solution.py:190
  35.3 35.3 %all_gather.21 = bf16[768,3,192]{2,1,0:T(4,128)(2,1)S(1)} all-gather(bf16[96,3,192]{2,1,0:T(4,128)(2,1)S(1)} %copy.82), channel_id=1, replica_groups=mesh['dp'=8,'tp'=4] {'dp'}, dimensions={0}, use_global_device_ids=true | all-gather | bytes 995328 | tf_op jit(solution)/shard_map/all_gather | solution.py:186
  70.6 2.1 copy.83
  72.6 2.0 fusion.107
  77.2 31.1 %all_gather.22 = bf16[192,768]{0,1:T(8,128)(2,1)S(1)} all-gather(bf16[192,96]{0,1:T(8,128)(2,1)S(1)} %copy.85), channel_id=1, replica_groups=mesh['dp'=8,'tp'=4] {'dp'}, dimensions={1}, use_global_device_ids=true | all-gather | bytes 331776 | tf_op jit(solution)/shard_map/all_gather | solution.py:187
  108.3 2.0 fusion.110
  114.5 1.6 fusion.133
  118.8 1.6 fusion.134
  120.4 1.6 convert_element_type.172
  122.1 1.6 convert_element_type.174
  124.4 64.3 %all-reduce.9.cloned.1.call-done = (f32[512,768]{1,0:T(8,128)}, f32[512,768]{1,0:T(8,128)}) async-done(((f32[512,768]{1,0:T(8,128)}, f32[512,768]{1,0:T(8,128)}), (f32[512,768]{1,0:T(8,128)}, f32[512,768]{1,0:T(8,128)})) %all-reduce.9.cloned.1.call-update) | async-done | bytes 3145744 | tf_op jit(solution)/shard_map/psum | solution.py:78
  188.7 3.0 fusion.123
  194.6 7.6 %multiply_convert_fusion.3 = (bf16[512,768]{1,0:T(8,128)(2,1)}, f32[512,768]{1,0:T(8,128)}, f32[512,768]{1,0:T(8,128)}) fusion(bf16[768,768]{1,0:T(8,128)(2,1)} %all-gather.4.cloned.1.call-done, f32[512,768]{1,0:T(8,128)} %copy-done.8, f32[768]{0:T(1024)} %get-tuple-element.39, f32[768]{0:T(1024)} %get-tuple-element.38, f32[512]{0:T(512)} %fusion.99, ...), kind=kOutput, calls=%fused_computation.98 | convolution fusion | flops 631504896 | bytes 6694912 | tf_op jit(solution)/shard_map/dot_general | solution.py:82
  202.2 4.3 all-gather.6.cloned.1.call-done
  206.5 3.6 add_convert_fusion.1
  211.0 2.0 fusion.135
  213.1 5.0 multiply_convert_fusion.2
  220.1 2.0 fusion.136
  222.3 1.3 log_add_fusion.1
  224.3 3.4 convolution_convert_fusion.1
  227.7 1.8 convolution_convert_fusion
  229.5 59.9 %all-reduce.7.cloned.1.call-done = (f32[512,768]{1,0:T(8,128)}, f32[512,768]{1,0:T(8,128)}) async-done(((f32[512,768]{1,0:T(8,128)}, f32[512,768]{1,0:T(8,128)}), (f32[512,768]{1,0:T(8,128)}, f32[512,768]{1,0:T(8,128)})) %all-reduce.7.cloned.1.call-update) | async-done | bytes 3145744 | tf_op jit(solution)/shard_map/psum | solution.py:93
  289.4 4.7 multiply_reduce_fusion.3
  294.2 1.4 fusion.120
  307.9 1.7 bitcast_convert_fusion.1
  309.7 1.7 bitcast_convert_fusion
  312.8 3.5 fusion.112
  319.4 61.3 %all-reduce.11.cloned.1.call-done = (bf16[512,768]{1,0:T(8,128)(2,1)}, bf16[512,768]{1,0:T(8,128)(2,1)}, bf16[512,768]{1,0:T(8,128)(2,1)}, bf16[512,768]{1,0:T(8,128)(2,1)}) async-done(((bf16[512,768]{1,0:T(8,128)(2,1)}, bf16[512,768]{1,0:T(8,128)(2,1)}, bf16[512,768]{1,0:T(8,128)(2,1)}, bf16[512,768]{1,0:T(8,128)(2,1)}), (bf16[512,768]{1,0:T(8,128)(2,1)}, bf16[512,768]{1,0:T(8,128)(2,1)}, ...) | async-done | bytes 3145744 | tf_op jit(solution)/shard_map/psum | solution.py:85
  380.8 2.5 fusion.9
  383.5 2.5 fusion.12
  387.2 4.4 convolution_add_fusion.1
  391.7 2.3 fusion.78
  394.1 2.3 convolution_add_fusion
  397.3 2.1 fusion.71
  399.5 2.5 convolution_add_fusion.2
  403.8 2.8 add_bitcast_fusion.1
  407.6 1.9 pad_maximum_fusion
  411.7 37.1 %reduce-scatter.18.cloned.1.call-done = f32[96,4]{1,0:T(8,128)} async-done(((f32[768,4]{1,0:T(8,128)}), f32[96,4]{1,0:T(8,128)}) %reduce-scatter.18.cloned.1.call-update) | async-done | bytes 1552
  450.9 70.0 %reduce-scatter.12.cloned.1.call-done = f32[96,768]{1,0:T(8,128)} async-done(((f32[768,768]{1,0:T(8,128)}), f32[96,768]{1,0:T(8,128)}) %reduce-scatter.12.cloned.1.call-update) | async-done | bytes 294928 | tf_op jit(solution)/shard_map/reduce_scatter | solution.py:198
  521.0 1.6 multiply_reduce_fusion.9
  522.6 70.3 %reduce-scatter.14.cloned.1.call-done = f32[768,96]{0,1:T(8,128)} async-done(((f32[768,768]{0,1:T(8,128)}), f32[768,96]{0,1:T(8,128)}) %reduce-scatter.14.cloned.1.call-update) | async-done | bytes 294928 | tf_op jit(solution)/shard_map/reduce_scatter | solution.py:199
  593.0 1.6 multiply_reduce_fusion.8
  594.6 70.2 %reduce-scatter.10.cloned.1.call-done = f32[96,3,192]{2,0,1:T(8,128)} async-done(((f32[768,3,192]{2,0,1:T(8,128)}), f32[96,3,192]{2,0,1:T(8,128)}) %reduce-scatter.10.cloned.1.call-update) | async-done | bytes 221200 | tf_op jit(solution)/shard_map/reduce_scatter | solution.py:196
  664.8 1.6 multiply_reduce_fusion.10
  669.1 1.3 pad_maximum_fusion.1
  670.4 39.6 %psum.71 = f32[]{:T(128)} all-reduce(f32[]{:T(128)S(6)} %add.323), channel_id=1, replica_groups=mesh['dp'=8,'tp'=4] {'dp','tp'}, use_global_device_ids=true, to_apply=%region_53.54 | all-reduce | flops 1 | bytes 8 | tf_op jit(solution)/shard_map/psum | solution.py:214
  (393 shorter events, 47.9 us)
Async XLA Ops:
  8.0 180.7 %all-reduce.9.cloned.1.call-start = ((), (), s32[]{:S(2)}) async-start(), calls=%async_computation.13 | async-start | bytes 6291456 | tf_op jit(solution)/shard_map/psum | solution.py:78
  9.0 26.1 %copy-start.38 = (f32[96,3,192]{2,0,1:T(8,128)S(1)}, f32[96,3,192]{2,0,1:T(8,128)}, u32[]{:S(2)}) copy-start(f32[96,3,192]{2,0,1:T(8,128)} %param.23) | copy-start | bytes 663556
  10.8 61.8 %copy-start.85 = (f32[512]{0:T(512)}, f32[512]{0:T(512)S(1)}, u32[]{:S(2)}) copy-start(f32[512]{0:T(512)S(1)} %get-tuple-element.109) | copy-start | bytes 6148
  10.9 97.4 %copy-start.83 = (f32[512]{0:T(512)}, f32[512]{0:T(512)S(1)}, u32[]{:S(2)}) copy-start(f32[512]{0:T(512)S(1)} %get-tuple-element.108) | copy-start | bytes 6148
  12.1 22.4 %copy-start.118 = (f32[512]{0:T(512)}, f32[512]{0:T(512)S(1)}, u32[]{:S(2)}) copy-start(f32[512]{0:T(512)S(1)} %get-tuple-element.32) | copy-start | bytes 6148
  12.1 60.5 %copy-start.104 = (f32[512]{0:T(512)}, f32[512]{0:T(512)S(1)}, u32[]{:S(2)}) copy-start(f32[512]{0:T(512)S(1)} %fusion.98) | copy-start | bytes 6148
  35.1 37.5 %copy-start.136 = (f32[768]{0:T(1024)}, f32[768]{0:T(1024)S(1)}, u32[]{:S(2)}) copy-start(f32[768]{0:T(1024)S(1)} %get-tuple-element.40) | copy-start | bytes 9220
  35.1 73.2 %copy-start.75 = (f32[768]{0:T(1024)}, f32[768]{0:T(1024)S(1)}, u32[]{:S(2)}) copy-start(f32[768]{0:T(1024)S(1)} %get-tuple-element.41) | copy-start | bytes 9220
  74.7 33.6 %copy-start.120 = (f32[512]{0:T(512)S(1)}, f32[512]{0:T(512)}, u32[]{:S(2)}) copy-start(f32[512]{0:T(512)} %get-tuple-element.33) | copy-start | bytes 6148
  75.5 35.8 %copy-start.32 = (bf16[1,512,192]{1,2,0:T(8,128)(2,1)}, bf16[1,512,192]{1,2,0:T(8,128)(2,1)S(1)}, u32[]{:S(2)}) copy-start(bf16[1,512,192]{1,2,0:T(8,128)(2,1)S(1)} %get-tuple-element.84) | copy-start | bytes 589828
  75.5 35.8 %copy-start.34 = (bf16[1,512,192]{1,2,0:T(8,128)(2,1)}, bf16[1,512,192]{1,2,0:T(8,128)(2,1)S(1)}, u32[]{:S(2)}) copy-start(bf16[1,512,192]{1,2,0:T(8,128)(2,1)S(1)} %get-tuple-element.83) | copy-start | bytes 589828
  110.5 5.5 copy-start.28
  110.5 5.5 copy-start.30
  110.6 6.7 copy-start.45
  120.4 74.2 %all-gather.4.cloned.1.call-start = ((), (), s32[]{:S(2)}) async-start(), calls=%async_computation.5 | async-start | bytes 1327104 | tf_op jit(solution)/shard_map/all_gather | solution.py:188
  122.1 84.4 %all-gather.6.cloned.1.call-start = ((), (), s32[]{:S(2)}) async-start(), calls=%async_computation.6 | async-start | bytes 1327104 | tf_op jit(solution)/shard_map/all_gather | solution.py:189
  123.8 165.6 %all-reduce.7.cloned.1.call-start = ((), (), s32[]{:S(2)}) async-start(), calls=%async_computation.12 | async-start | bytes 6291456 | tf_op jit(solution)/shard_map/psum | solution.py:93
  213.0 5.0 copy-start.12
  213.0 5.0 copy-start.141
  222.1 158.7 %all-reduce.11.cloned.1.call-start = ((), (), s32[]{:S(2)}) async-start(), calls=%async_computation.14 | async-start | bytes 6291456 | tf_op jit(solution)/shard_map/psum | solution.py:85
  297.3 5.8 copy-start.22
  301.8 5.5 copy-start.68
  311.5 4.9 copy-start.128
  311.5 4.9 copy-start.25
  311.5 4.9 copy-start.52
  311.5 90.5 %reduce-scatter.16.cloned.1.call-start = ((), (), s32[]{:S(2)}) async-start(), calls=%async_computation.10 | async-start | bytes 884736
  318.1 62.6 %copy-start.3 = (bf16[2,512,768]{2,1,0:T(8,128)(2,1)S(1)}, bf16[2,512,768]{2,1,0:T(8,128)(2,1)}, u32[]{:S(2)}) copy-start(bf16[2,512,768]{2,1,0:T(8,128)(2,1)} %param.19) | copy-start | bytes 4718596
  318.1 62.6 %copy-start.76 = (f32[768]{0:T(1024)S(1)}, f32[768]{0:T(1024)}, u32[]{:S(2)}) copy-start(f32[768]{0:T(1024)} %copy-done.75) | copy-start | bytes 9220
  318.2 62.6 %copy-start.84 = (f32[512]{0:T(512)S(1)}, f32[512]{0:T(512)}, u32[]{:S(2)}) copy-start(f32[512]{0:T(512)} %copy-done.83) | copy-start | bytes 6148
  318.2 62.6 %copy-start.86 = (f32[512]{0:T(512)S(1)}, f32[512]{0:T(512)}, u32[]{:S(2)}) copy-start(f32[512]{0:T(512)} %copy-done.85) | copy-start | bytes 6148
  319.4 129.4 %reduce-scatter.18.cloned.1.call-start = ((), (), s32[]{:S(2)}) async-start(), calls=%async_computation.11 | async-start | bytes 442368
  387.1 133.9 %reduce-scatter.12.cloned.1.call-start = ((), (), s32[]{:S(2)}) async-start(), calls=%async_computation.8 | async-start | bytes 2654208 | tf_op jit(solution)/shard_map/reduce_scatter | solution.py:198
  391.6 201.4 %reduce-scatter.14.cloned.1.call-start = ((), (), s32[]{:S(2)}) async-start(), calls=%async_computation.9 | async-start | bytes 2654208 | tf_op jit(solution)/shard_map/reduce_scatter | solution.py:199
  396.3 268.4 %reduce-scatter.10.cloned.1.call-start = ((), (), s32[]{:S(2)}) async-start(), calls=%async_computation.7 | async-start | bytes 2654208 | tf_op jit(solution)/shard_map/reduce_scatter | solution.py:196
  669.0 41.7 %copy-start.135 = (f32[4,96]{1,0:T(4,128)S(1)}, f32[4,96]{1,0:T(4,128)}, u32[]{:S(2)}) copy-start(f32[4,96]{1,0:T(4,128)} %param.27) | copy-start | bytes 4612
  669.0 41.7 %copy-start.139 = (f32[4,96]{1,0:T(4,128)S(1)}, f32[4,96]{1,0:T(4,128)}, u32[]{:S(2)}) copy-start(f32[4,96]{1,0:T(4,128)} %param.32) | copy-start | bytes 4612
  669.0 41.7 %copy-start.140 = (f32[4,96]{1,0:T(4,128)S(1)}, f32[4,96]{1,0:T(4,128)}, u32[]{:S(2)}) copy-start(f32[4,96]{1,0:T(4,128)} %param.37) | copy-start | bytes 4612
  669.0 42.3 %copy-start.59 = (f32[192,96]{1,0:T(8,128)S(1)}, f32[192,96]{1,0:T(8,128)}, u32[]{:S(2)}) copy-start(f32[192,96]{1,0:T(8,128)} %param.24) | copy-start | bytes 221188
  669.0 42.3 %copy-start.77 = (f32[192,96]{1,0:T(8,128)S(1)}, f32[192,96]{1,0:T(8,128)}, u32[]{:S(2)}) copy-start(f32[192,96]{1,0:T(8,128)} %param.29) | copy-start | bytes 221188
  669.1 42.3 %copy-start.78 = (f32[192,96]{1,0:T(8,128)S(1)}, f32[192,96]{1,0:T(8,128)}, u32[]{:S(2)}) copy-start(f32[192,96]{1,0:T(8,128)} %param.34) | copy-start | bytes 221188
  669.1 43.0 %copy-start.36 = (f32[768,96]{0,1:T(8,128)S(1)}, f32[768,96]{0,1:T(8,128)}, u32[]{:S(2)}) copy-start(f32[768,96]{0,1:T(8,128)} %param.26) | copy-start | bytes 884740
  669.1 43.0 %copy-start.41 = (f32[768,96]{0,1:T(8,128)S(1)}, f32[768,96]{0,1:T(8,128)}, u32[]{:S(2)}) copy-start(f32[768,96]{0,1:T(8,128)} %reduce-scatter.14.cloned.1.call-done) | copy-start | bytes 884740
  669.1 43.0 %copy-start.60 = (f32[768,96]{0,1:T(8,128)S(1)}, f32[768,96]{0,1:T(8,128)}, u32[]{:S(2)}) copy-start(f32[768,96]{0,1:T(8,128)} %param.31) | copy-start | bytes 884740
  669.1 43.0 %copy-start.61 = (f32[768,96]{0,1:T(8,128)S(1)}, f32[768,96]{0,1:T(8,128)}, u32[]{:S(2)}) copy-start(f32[768,96]{0,1:T(8,128)} %param.36) | copy-start | bytes 884740
  670.4 42.8 %copy-start.37 = (f32[96,768]{1,0:T(8,128)S(1)}, f32[96,768]{1,0:T(8,128)}, u32[]{:S(2)}) copy-start(f32[96,768]{1,0:T(8,128)} %param.25) | copy-start | bytes 884740
  670.4 42.8 %copy-start.40 = (f32[96,768]{1,0:T(8,128)S(1)}, f32[96,768]{1,0:T(8,128)}, u32[]{:S(2)}) copy-start(f32[96,768]{1,0:T(8,128)} %reduce-scatter.12.cloned.1.call-done) | copy-start | bytes 884740
  670.4 42.8 %copy-start.62 = (f32[96,768]{1,0:T(8,128)S(1)}, f32[96,768]{1,0:T(8,128)}, u32[]{:S(2)}) copy-start(f32[96,768]{1,0:T(8,128)} %param.30) | copy-start | bytes 884740
  670.4 42.8 %copy-start.63 = (f32[96,768]{1,0:T(8,128)S(1)}, f32[96,768]{1,0:T(8,128)}, u32[]{:S(2)}) copy-start(f32[96,768]{1,0:T(8,128)} %param.35) | copy-start | bytes 884740
  (107 other events, 259.9 us)
Sparse Core Ops, SparseCore 0:
  120.5 68.1 all-reduce.8
  222.2 67.1 all-reduce.6
  311.6 69.1 all-reduce.10
Sparse Core Ops, SparseCore 1:
  123.6 40.9 all-gather.3
  166.6 39.9 all-gather.5
  319.5 62.4 reduce-scatter.15
  387.2 61.6 reduce-scatter.17
  452.7 68.2 reduce-scatter.11
  524.9 68.0 reduce-scatter.13
  596.7 68.0 reduce-scatter.9
where the time goes:
time: 731 us; the launch traced here: 724 us
  waiting for transfers between devices  438 us (60%)
  blocking collectives  128 us (18%)
  matrix products  63.2 us (9%)
  other arithmetic  47.9 us (7%)
  local copies, waits for them, and re-layouts  22.8 us (3%)
  between operations  22.4 us (3%)
    reduce_scatter x1, waiting for transfers between devices, local(): lax.psum_scatter(grad_list[3], 'dp', scatter_dimension=1, tiled=True)  70.3 us
    reduce_scatter x1, waiting for transfers between devices, local(): lax.psum_scatter(grad_list[0], 'dp', scatter_dimension=0, tiled=True)  70.2 us
    reduce_scatter x1, waiting for transfers between devices, local(): lax.psum_scatter(grad_list[2], 'dp', scatter_dimension=0, tiled=True)  70 us
    psum x1, waiting for transfers between devices, one_micro(): lax.psum(jnp.dot(context, out_mat, preferred_element_type=jnp.float32), '...  64.3 us
    psum x1, waiting for transfers between devices, one_micro(): lax.psum(jnp.dot(hidden, down_mat, preferred_element_type=jnp.float32).as...  61.3 us
    psum x1, waiting for transfers between devices, one_micro(): lax.psum(jnp.einsum('tf,df->td', grad_pre, up_mat, preferred_element_type...  59.9 us
    psum x1, blocking collectives, local(): grad_norm = jnp.sqrt(lax.psum(own_squares, ('dp', 'tp')))  39.6 us
    unnamed x12, waiting for transfers between devices  37.3 us
  transfers between devices with their start and end apart: 10, of which 8 were waited for; matrix products, arithmetic and copies ran while one was open for 8% of the time, Pallas kernels for 0%

commit v1 on v0

--- a/solution.py
+++ b/solution.py
@@ -14,6 +14,19 @@
 beta_two = 0.999
 adam_eps = 1e-08
 weight_decay = 0.01
+
+
+def gather_around(shard, axis, dim):
+    count, position, rows = (lax.axis_size(axis), lax.axis_index(axis), shard.shape[dim])
+    upward = [(i, (i + 1) % count) for i in range(count)]
+    whole = jnp.zeros((*shard.shape[:dim], count * rows, *shard.shape[dim + 1 :]), shard.dtype)
+    carried = shard
+    for step in range(count):
+        source = (position - step) % count
+        whole = lax.dynamic_update_slice_in_dim(whole, carried, source * rows, axis=dim)
+        if step < count - 1:
+            carried = lax.ppermute(carried, axis, upward)
+    return whole
 
 
 def time_embed(step_values, model_width):
@@ -184,7 +197,7 @@
     for number in range(micro_count):
         gathered = (
             lax.all_gather(qkv_low, "dp", axis=0, tiled=True),
-            lax.all_gather(out_low, "dp", axis=1, tiled=True),
+            gather_around(out_low, "dp", 1),
             lax.all_gather(up_low, "dp", axis=0, tiled=True),
             lax.all_gather(down_low, "dp", axis=1, tiled=True),
             lax.all_gather(norm_low, "dp", axis=1, tiled=True),

time: 731 us -> 746 us (1.021)
  waiting for transfers between devices: 438 us -> 480 us
  blocking collectives: 128 us -> 93.9 us
    ppermute x0 -> x7, waiting for transfers between devices: none -> 32.1 us  [gather_around(): carried = lax.ppermute(carried, axis, upward)]
    all_gather x1 -> x0, blocking collectives: 31.1 us -> none  [local(): lax.all_gather(out_low, 'dp', axis=1, tiled=True)]
    dynamic_update_slice x0 -> x8, local copies, waits for them, and re-layouts: none -> 8.71 us  [gather_around(): lax.dynamic_update_slice_in_dim(whole, carried, source * rows, axis=dim)]
    unnamed x295 -> x200, local copies, waits for them, and re-layouts: 19.1 us -> 17.7 us
  transfers between devices with their start and end apart: 10 -> 17, of which waited for: 8 -> 13; matrix products, arithmetic and copies ran while one was open for 8% -> 11% of each run, Pallas kernels for 0% -> 0%
where the time goes in v1:
time: 746 us; the launch traced here: 738 us
  waiting for transfers between devices  480 us (64%)
  blocking collectives  93.9 us (13%)
  matrix products  64.2 us (9%)
  other arithmetic  44.8 us (6%)
  local copies, waits for them, and re-layouts  28.9 us (4%)
  between operations  22 us (3%)
    psum x1, waiting for transfers between devices, one_micro(): lax.psum(jnp.dot(context, out_mat, preferred_element_type=jnp.float32), '...  71.1 us
    reduce_scatter x1, waiting for transfers between devices, local(): lax.psum_scatter(grad_list[3], 'dp', scatter_dimension=1, tiled=True)  70.4 us
    reduce_scatter x1, waiting for transfers between devices, local(): lax.psum_scatter(grad_list[0], 'dp', scatter_dimension=0, tiled=True)  70.2 us
    reduce_scatter x1, waiting for transfers between devices, local(): lax.psum_scatter(grad_list[2], 'dp', scatter_dimension=0, tiled=True)  69.8 us
    psum x1, waiting for transfers between devices, one_micro(): lax.psum(jnp.einsum('tf,df->td', grad_pre, up_mat, preferred_element_type...  62 us
    psum x1, waiting for transfers between devices, one_micro(): lax.psum(jnp.dot(hidden, down_mat, preferred_element_type=jnp.float32).as...  61.1 us
    psum x1, blocking collectives, local(): grad_norm = jnp.sqrt(lax.psum(own_squares, ('dp', 'tp')))  39.6 us
    unnamed x12, waiting for transfers between devices  37.5 us
  transfers between devices with their start and end apart: 17, of which 13 were waited for; matrix products, arithmetic and copies ran while one was open for 11% of the time, Pallas kernels for 0%

profile of v1, /device:TPU:0, one launch (start us, length us, event | category | flops | bytes accessed | tf_op | source)
XLA Modules:
  0.0 738.2 jit_solution(9832678539348935529)
XLA Ops:
  9.1 2.9 collective-permute-start
  12.9 1.8 fusion.30
  15.4 19.3 %all-gather = bf16[8,96,4]{1,2,0:T(4,128)(2,1)S(1)} all-gather(bf16[1,96,4]{1,2,0:T(4,128)(2,1)S(1)} %convert_bitcast_fusion.2), channel_id=1, replica_groups=mesh['dp'=8,'tp'=4] {'dp'}, dimensions={0}, use_global_device_ids=true | all-gather | bytes 6912 | tf_op jit(solution)/shard_map/all_gather | solution.py:203
  35.6 35.0 %all_gather.17 = bf16[768,3,192]{2,1,0:T(4,128)(2,1)S(1)} all-gather(bf16[96,3,192]{2,1,0:T(4,128)(2,1)S(1)} %copy.81), channel_id=1, replica_groups=mesh['dp'=8,'tp'=4] {'dp'}, dimensions={0}, use_global_device_ids=true | all-gather | bytes 995328 | tf_op jit(solution)/shard_map/all_gather | solution.py:199
  70.6 2.1 copy.82
  72.7 2.0 fusion.107
  80.0 6.4 collective-permute-done.1
  86.5 6.7 collective-permute-done.2
  93.4 6.6 collective-permute-done.3
  100.8 5.9 collective-permute-done.4
  107.2 6.5 collective-permute-done.5
  124.3 2.6 fusion.133
  128.6 1.6 convert_element_type.172
  130.3 1.6 convert_element_type.174
  132.0 71.1 %all-reduce.9.cloned.1.call-done = (f32[512,768]{1,0:T(8,128)}, f32[512,768]{1,0:T(8,128)}) async-done(((f32[512,768]{1,0:T(8,128)}, f32[512,768]{1,0:T(8,128)}), (f32[512,768]{1,0:T(8,128)}, f32[512,768]{1,0:T(8,128)})) %all-reduce.9.cloned.1.call-update) | async-done | bytes 3145744 | tf_op jit(solution)/shard_map/psum | solution.py:91
  203.1 3.0 fusion.123
  207.8 7.5 %multiply_convert_fusion.3 = (bf16[512,768]{1,0:T(8,128)(2,1)}, f32[512,768]{1,0:T(8,128)}, f32[512,768]{1,0:T(8,128)}) fusion(bf16[768,768]{1,0:T(8,128)(2,1)} %all-gather.4.cloned.1.call-done, f32[512,768]{1,0:T(8,128)} %copy-done.9, f32[768]{0:T(1024)S(1)} %copy-done.86, f32[768]{0:T(1024)S(1)} %get-tuple-element.38, f32[512]{0:T(512)S(1)} %fusion.99, ...), kind=kOutput, calls=%fused_computation.98 | convolution fusion | flops 631504896 | bytes 6694912 | tf_op jit(solution)/shard_map/dot_general | solution.py:95
  215.4 5.5 all-gather.6.cloned.1.call-done
  220.9 3.6 add_convert_fusion.1
  225.4 2.0 fusion.135
  227.4 5.0 multiply_convert_fusion.2
  234.4 2.0 fusion.136
  236.7 3.3 convolution_convert_fusion.1
  240.0 1.7 convolution_convert_fusion
  241.7 62.0 %all-reduce.7.cloned.1.call-done = (f32[512,768]{1,0:T(8,128)}, f32[512,768]{1,0:T(8,128)}) async-done(((f32[512,768]{1,0:T(8,128)}, f32[512,768]{1,0:T(8,128)}), (f32[512,768]{1,0:T(8,128)}, f32[512,768]{1,0:T(8,128)})) %all-reduce.7.cloned.1.call-update) | async-done | bytes 3145744 | tf_op jit(solution)/shard_map/psum | solution.py:106
  303.7 3.8 multiply_reduce_fusion.3
  321.9 1.7 bitcast_convert_fusion.1
  323.7 1.7 bitcast_convert_fusion
  326.8 3.5 fusion.112
  333.6 61.1 %all-reduce.11.cloned.1.call-done = (bf16[512,768]{1,0:T(8,128)(2,1)}, bf16[512,768]{1,0:T(8,128)(2,1)}, bf16[512,768]{1,0:T(8,128)(2,1)}, bf16[512,768]{1,0:T(8,128)(2,1)}) async-done(((bf16[512,768]{1,0:T(8,128)(2,1)}, bf16[512,768]{1,0:T(8,128)(2,1)}, bf16[512,768]{1,0:T(8,128)(2,1)}, bf16[512,768]{1,0:T(8,128)(2,1)}), (bf16[512,768]{1,0:T(8,128)(2,1)}, bf16[512,768]{1,0:T(8,128)(2,1)}, ...) | async-done | bytes 3145744 | tf_op jit(solution)/shard_map/psum | solution.py:98
  394.8 2.5 fusion.9
  397.4 2.0 fusion.12
  400.5 4.3 convolution_add_fusion.1
  404.9 2.4 fusion.78
  407.3 2.2 convolution_add_fusion
  410.5 2.1 fusion.71
  412.7 2.5 convolution_add_fusion.2
  416.9 2.8 add_bitcast_fusion.1
  420.8 1.9 pad_maximum_fusion
  424.9 37.3 %reduce-scatter.18.cloned.1.call-done = f32[96,4]{1,0:T(8,128)} async-done(((f32[768,4]{1,0:T(8,128)}), f32[96,4]{1,0:T(8,128)}) %reduce-scatter.18.cloned.1.call-update) | async-done | bytes 1552
  464.3 69.8 %reduce-scatter.12.cloned.1.call-done = f32[96,768]{1,0:T(8,128)} async-done(((f32[768,768]{1,0:T(8,128)}), f32[96,768]{1,0:T(8,128)}) %reduce-scatter.12.cloned.1.call-update) | async-done | bytes 294928 | tf_op jit(solution)/shard_map/reduce_scatter | solution.py:211
  534.1 1.6 multiply_reduce_fusion.9
  535.7 70.4 %reduce-scatter.14.cloned.1.call-done = f32[768,96]{0,1:T(8,128)} async-done(((f32[768,768]{0,1:T(8,128)}), f32[768,96]{0,1:T(8,128)}) %reduce-scatter.14.cloned.1.call-update) | async-done | bytes 294928 | tf_op jit(solution)/shard_map/reduce_scatter | solution.py:212
  606.2 1.6 multiply_reduce_fusion.8
  607.8 70.2 %reduce-scatter.10.cloned.1.call-done = f32[96,3,192]{2,0,1:T(8,128)} async-done(((f32[768,3,192]{2,0,1:T(8,128)}), f32[96,3,192]{2,0,1:T(8,128)}) %reduce-scatter.10.cloned.1.call-update) | async-done | bytes 221200 | tf_op jit(solution)/shard_map/reduce_scatter | solution.py:209
  678.0 1.6 multiply_reduce_fusion.10
  683.7 39.6 %psum.71 = f32[]{:T(128)} all-reduce(f32[]{:T(128)S(6)} %add.411), channel_id=1, replica_groups=mesh['dp'=8,'tp'=4] {'dp','tp'}, use_global_device_ids=true, to_apply=%region_53.54 | all-reduce | flops 1 | bytes 8 | tf_op jit(solution)/shard_map/psum | solution.py:227
  725.4 2.1 multiply_subtract_fusion
  (321 shorter events, 59.3 us)
Async XLA Ops:
  8.0 6.7 copy-start.2
  8.0 195.1 %all-reduce.9.cloned.1.call-start = ((), (), s32[]{:S(2)}) async-start(), calls=%async_computation.13 | async-start | bytes 6291456 | tf_op jit(solution)/shard_map/psum | solution.py:91
  9.1 70.4 %collective-permute-start = (bf16[192,96]{1,0:T(8,128)(2,1)S(1)}, bf16[192,96]{1,0:T(8,128)(2,1)S(1)}, u32[]{:S(2)}, u32[]{:S(2)}) collective-permute-start(bf16[192,96]{1,0:T(8,128)(2,1)S(1)} %convert_element_type.170), channel_id=1, source_target_pairs={{0,4},{4,8},{8,12},{12,16},{16,20},{20,24},{24,28},{28,0},{1,5},{5... | collective-permute-start | bytes 110600 | tf_op jit(solution)/shard_map/ppermute | solution.py:28
  12.9 22.6 %copy-start.40 = (f32[96,3,192]{2,0,1:T(8,128)S(1)}, f32[96,3,192]{2,0,1:T(8,128)}, u32[]{:S(2)}) copy-start(f32[96,3,192]{2,0,1:T(8,128)} %param.23) | copy-start | bytes 663556
  15.4 57.4 %copy-start.82 = (f32[512]{0:T(512)}, f32[512]{0:T(512)S(1)}, u32[]{:S(2)}) copy-start(f32[512]{0:T(512)S(1)} %get-tuple-element.32) | copy-start | bytes 6148
  15.4 60.3 %copy-start.84 = (f32[512]{0:T(512)}, f32[512]{0:T(512)S(1)}, u32[]{:S(2)}) copy-start(f32[512]{0:T(512)S(1)} %get-tuple-element.33) | copy-start | bytes 6148
  35.4 42.9 %copy-start.89 = (f32[768]{0:T(1024)}, f32[768]{0:T(1024)S(1)}, u32[]{:S(2)}) copy-start(f32[768]{0:T(1024)S(1)} %get-tuple-element.40) | copy-start | bytes 9220
  79.5 13.9 %copy-start.77 = (bf16[192,96]{1,0:T(8,128)(2,1)}, bf16[192,96]{1,0:T(8,128)(2,1)S(1)}, u32[]{:S(2)}) copy-start(bf16[192,96]{1,0:T(8,128)(2,1)S(1)} %collective-permute-done) | copy-start | bytes 110596
  79.5 6.8 collective-permute-start.1
  86.4 14.4 %copy-start.78 = (bf16[192,96]{1,0:T(8,128)(2,1)}, bf16[192,96]{1,0:T(8,128)(2,1)S(1)}, u32[]{:S(2)}) copy-start(bf16[192,96]{1,0:T(8,128)(2,1)S(1)} %collective-permute-done.1) | copy-start | bytes 110596
  86.4 6.8 collective-permute-start.2
  86.4 14.3 %copy-start.34 = (bf16[1,512,192]{1,2,0:T(8,128)(2,1)}, bf16[1,512,192]{1,2,0:T(8,128)(2,1)S(1)}, u32[]{:S(2)}) copy-start(bf16[1,512,192]{1,2,0:T(8,128)(2,1)S(1)} %get-tuple-element.87) | copy-start | bytes 589828
  86.4 14.3 %copy-start.36 = (bf16[1,512,192]{1,2,0:T(8,128)(2,1)}, bf16[1,512,192]{1,2,0:T(8,128)(2,1)S(1)}, u32[]{:S(2)}) copy-start(bf16[1,512,192]{1,2,0:T(8,128)(2,1)S(1)} %get-tuple-element.86) | copy-start | bytes 589828
  86.5 27.6 %copy-start.49 = (bf16[1,512,192]{1,2,0:T(8,128)(2,1)}, bf16[1,512,192]{1,2,0:T(8,128)(2,1)S(1)}, u32[]{:S(2)}) copy-start(bf16[1,512,192]{1,2,0:T(8,128)(2,1)S(1)} %get-tuple-element.88) | copy-start | bytes 589828
  93.2 7.6 %copy-start.79 = (bf16[192,96]{1,0:T(8,128)(2,1)}, bf16[192,96]{1,0:T(8,128)(2,1)S(1)}, u32[]{:S(2)}) copy-start(bf16[192,96]{1,0:T(8,128)(2,1)S(1)} %collective-permute-done.2) | copy-start | bytes 110596
  93.2 6.8 collective-permute-start.3
  100.0 6.8 collective-permute-start.4
  100.8 13.3 %copy-start = (f32[3,512,512]{1,2,0:T(8,128)}, f32[3,512,512]{1,2,0:T(8,128)S(1)}, u32[]{:S(2)}) copy-start(f32[3,512,512]{1,2,0:T(8,128)S(1)} %get-tuple-element.99) | copy-start | bytes 9437188
  106.7 8.7 %copy-start.81 = (bf16[192,96]{1,0:T(8,128)(2,1)}, bf16[192,96]{1,0:T(8,128)(2,1)S(1)}, u32[]{:S(2)}) copy-start(bf16[192,96]{1,0:T(8,128)(2,1)S(1)} %collective-permute-done.4) | copy-start | bytes 110596
  106.8 6.9 collective-permute-start.5
  113.6 9.4 %collective-permute-start.6 = (bf16[192,96]{1,0:T(8,128)(2,1)}, bf16[192,96]{1,0:T(8,128)(2,1)}, u32[]{:S(2)}, u32[]{:S(2)}) collective-permute-start(bf16[192,96]{1,0:T(8,128)(2,1)} %collective-permute-done.5), channel_id=1, source_target_pairs={{0,4},{4,8},{8,12},{12,16},{16,20},{20,24},{24,28},{28,0},{1,5},{5... | collective-permute-start | bytes 110600 | tf_op jit(solution)/shard_map/ppermute | solution.py:28
  128.5 79.3 %all-gather.4.cloned.1.call-start = ((), (), s32[]{:S(2)}) async-start(), calls=%async_computation.5 | async-start | bytes 1327104 | tf_op jit(solution)/shard_map/all_gather | solution.py:201
  130.3 90.6 %all-gather.6.cloned.1.call-start = ((), (), s32[]{:S(2)}) async-start(), calls=%async_computation.6 | async-start | bytes 1327104 | tf_op jit(solution)/shard_map/all_gather | solution.py:202
  132.0 171.7 %all-reduce.7.cloned.1.call-start = ((), (), s32[]{:S(2)}) async-start(), calls=%async_computation.12 | async-start | bytes 6291456 | tf_op jit(solution)/shard_map/psum | solution.py:106
  236.4 158.4 %all-reduce.11.cloned.1.call-start = ((), (), s32[]{:S(2)}) async-start(), calls=%async_computation.14 | async-start | bytes 6291456 | tf_op jit(solution)/shard_map/psum | solution.py:98
  314.9 6.5 copy-start.69
  315.5 5.9 copy-start.70
  316.1 5.3 copy-start.65
  325.5 89.8 %reduce-scatter.16.cloned.1.call-start = ((), (), s32[]{:S(2)}) async-start(), calls=%async_computation.10 | async-start | bytes 884736
  332.1 62.6 %copy-start.4 = (bf16[2,512,768]{2,1,0:T(8,128)(2,1)S(1)}, bf16[2,512,768]{2,1,0:T(8,128)(2,1)}, u32[]{:S(2)}) copy-start(bf16[2,512,768]{2,1,0:T(8,128)(2,1)} %param.19) | copy-start | bytes 4718596
  333.3 128.8 %reduce-scatter.18.cloned.1.call-start = ((), (), s32[]{:S(2)}) async-start(), calls=%async_computation.11 | async-start | bytes 442368
  400.4 133.7 %reduce-scatter.12.cloned.1.call-start = ((), (), s32[]{:S(2)}) async-start(), calls=%async_computation.8 | async-start | bytes 2654208 | tf_op jit(solution)/shard_map/reduce_scatter | solution.py:211
  404.9 201.3 %reduce-scatter.14.cloned.1.call-start = ((), (), s32[]{:S(2)}) async-start(), calls=%async_computation.9 | async-start | bytes 2654208 | tf_op jit(solution)/shard_map/reduce_scatter | solution.py:212
  409.6 268.4 %reduce-scatter.10.cloned.1.call-start = ((), (), s32[]{:S(2)}) async-start(), calls=%async_computation.7 | async-start | bytes 2654208 | tf_op jit(solution)/shard_map/reduce_scatter | solution.py:209
  424.7 257.6 %copy-start.29 = (bf16[1,512,768]{2,1,0:T(8,128)(2,1)S(1)}, bf16[1,512,768]{2,1,0:T(8,128)(2,1)}, u32[]{:S(2)}) copy-start(bf16[1,512,768]{2,1,0:T(8,128)(2,1)} %fusion.68) | copy-start | bytes 2359300
  682.3 41.7 %copy-start.88 = (f32[4,96]{1,0:T(4,128)S(1)}, f32[4,96]{1,0:T(4,128)}, u32[]{:S(2)}) copy-start(f32[4,96]{1,0:T(4,128)} %param.27) | copy-start | bytes 4612
  682.3 41.7 %copy-start.92 = (f32[4,96]{1,0:T(4,128)S(1)}, f32[4,96]{1,0:T(4,128)}, u32[]{:S(2)}) copy-start(f32[4,96]{1,0:T(4,128)} %param.32) | copy-start | bytes 4612
  682.3 41.7 %copy-start.93 = (f32[4,96]{1,0:T(4,128)S(1)}, f32[4,96]{1,0:T(4,128)}, u32[]{:S(2)}) copy-start(f32[4,96]{1,0:T(4,128)} %param.37) | copy-start | bytes 4612
  682.3 42.3 %copy-start.59 = (f32[192,96]{1,0:T(8,128)S(1)}, f32[192,96]{1,0:T(8,128)}, u32[]{:S(2)}) copy-start(f32[192,96]{1,0:T(8,128)} %param.24) | copy-start | bytes 221188
  682.3 42.3 %copy-start.75 = (f32[192,96]{1,0:T(8,128)S(1)}, f32[192,96]{1,0:T(8,128)}, u32[]{:S(2)}) copy-start(f32[192,96]{1,0:T(8,128)} %param.29) | copy-start | bytes 221188
  682.3 42.3 %copy-start.76 = (f32[192,96]{1,0:T(8,128)S(1)}, f32[192,96]{1,0:T(8,128)}, u32[]{:S(2)}) copy-start(f32[192,96]{1,0:T(8,128)} %param.34) | copy-start | bytes 221188
  682.3 43.0 %copy-start.38 = (f32[768,96]{0,1:T(8,128)S(1)}, f32[768,96]{0,1:T(8,128)}, u32[]{:S(2)}) copy-start(f32[768,96]{0,1:T(8,128)} %param.26) | copy-start | bytes 884740
  682.4 43.0 %copy-start.43 = (f32[768,96]{0,1:T(8,128)S(1)}, f32[768,96]{0,1:T(8,128)}, u32[]{:S(2)}) copy-start(f32[768,96]{0,1:T(8,128)} %reduce-scatter.14.cloned.1.call-done) | copy-start | bytes 884740
  682.4 43.0 %copy-start.60 = (f32[768,96]{0,1:T(8,128)S(1)}, f32[768,96]{0,1:T(8,128)}, u32[]{:S(2)}) copy-start(f32[768,96]{0,1:T(8,128)} %param.31) | copy-start | bytes 884740
  683.7 43.9 %copy-start.39 = (f32[96,768]{1,0:T(8,128)S(1)}, f32[96,768]{1,0:T(8,128)}, u32[]{:S(2)}) copy-start(f32[96,768]{1,0:T(8,128)} %param.25) | copy-start | bytes 884740
  683.7 43.9 %copy-start.42 = (f32[96,768]{1,0:T(8,128)S(1)}, f32[96,768]{1,0:T(8,128)}, u32[]{:S(2)}) copy-start(f32[96,768]{1,0:T(8,128)} %reduce-scatter.12.cloned.1.call-done) | copy-start | bytes 884740
  683.7 43.9 %copy-start.61 = (f32[96,768]{1,0:T(8,128)S(1)}, f32[96,768]{1,0:T(8,128)}, u32[]{:S(2)}) copy-start(f32[96,768]{1,0:T(8,128)} %param.30) | copy-start | bytes 884740
  683.7 43.9 %copy-start.62 = (f32[96,768]{1,0:T(8,128)S(1)}, f32[96,768]{1,0:T(8,128)}, u32[]{:S(2)}) copy-start(f32[96,768]{1,0:T(8,128)} %param.35) | copy-start | bytes 884740
  (67 other events, 157.9 us)
Sparse Core Ops, SparseCore 0:
  128.7 74.3 all-reduce.8
  236.5 67.1 all-reduce.6
  325.6 69.1 all-reduce.10
Sparse Core Ops, SparseCore 1:
  131.8 47.0 all-gather.3
  180.9 39.9 all-gather.5
  333.4 62.4 reduce-scatter.15
  400.5 61.6 reduce-scatter.17
  466.1 68.0 reduce-scatter.11
  538.0 68.1 reduce-scatter.13
  609.9 68.0 reduce-scatter.9
